TPU v7x, 256 devices: a whole 4x4x8 slice. The times are simulated.
256 devices in a mesh: corpus: 64 (over x, z, core), rep: 4 (over y).
Axes of the slice: x: 4, y: 4, z: 8, core: 2. Of those that a mesh axis runs over, the one named last changes fastest.
Arguments:
- queries: bfloat16 [32768, 768], P(('corpus', 'rep')), may hold values from -18 to 18
- teacher: float32 [32768, 64], P(('corpus', 'rep')), may hold values from -15 to 305
- slab: bfloat16 [65536, 768], P('corpus'), may hold values from -12 to 12
- candidates: int32 [32768, 64], P(('corpus', 'rep')), may hold values from 0 to 65535, as said below
- hot_ids: int32 [2048], replicated, may hold values from 0 to 65535, as said below
- location: int32 [65536], replicated, may hold values from 0 to 65535, as said below
Outputs:
- loss: float32 [32768], P(('corpus', 'rep'))
- query_grad: float32 [32768, 768], P(('corpus', 'rep'))
- slab_grad: float32 [65536, 768], P(('corpus', 'rep'))
Inputs may be any that keep to these rules, and one draw needn't show every extreme that they name: `candidates`: every query names 64 passage ids, exactly 8 of them absent from hot_ids; ids may repeat. With the owner of id p being location[p] // 1024, the ids absent from hot_ids among one device's 128 queries (aligned blocks of 128 rows) fall at most 24 times on any owner; in each block some owner gets exactly 24, the same owner for all blocks whose block number has the same remainder modulo the number of rep devices. `hot_ids`: 2048 distinct ids; entries 32 * c to 32 * c + 31 are owned by corpus index c. `location`: A permutation of the passage ids onto slab rows.
All inputs are finite; a program needn't handle non-finite values.
Results may differ from a plain program's by a relative error of at most 0.0026.
Values may be sent and summed in bfloat16 or wider, within the bound.
No kernel may reach another device: no remote copies, remote signals or barrier semaphores. Data moves between devices by JAX's collectives and lax.ppermute only.
A program may use at most 128 MiB of HBM per device.

v0:
```python
import functools
import math

import jax
import jax.numpy as jnp
from jax import lax
from jax.experimental import pallas as pl
from jax.experimental.pallas import tpu as pltpu
from jax.sharding import PartitionSpec as P


COLD = 8
LANES = 128
RADIX = 256
F32 = jnp.float32
BF16 = jnp.bfloat16
VMEM_SPEC = pl.BlockSpec(memory_space=pltpu.VMEM)
SMEM_SPEC = pl.BlockSpec(memory_space=pltpu.SMEM)
ROWS_DOT = (((1,), (1,)), ((), ()))


def iota(shape, axis):
    return lax.broadcasted_iota(jnp.int32, shape, axis)


def one_hot(mask, dtype=BF16):
    return jnp.where(mask, 1.0, 0.0).astype(dtype)


def pick_rows(mask, values):
    return jnp.sum(jnp.where(mask, values, jnp.zeros_like(values)), axis=0, keepdims=True)


def request_kernel(per_owner, groups, cand_t, hot_ref, loc_ref, req_ref, place_ref, sel_ref, hit_t):
    cand_count, q_rows = cand_t.shape
    hot_total = hot_ref.shape[1]
    high_rows = loc_ref.shape[0] // 2
    hot = hot_ref[...]
    low_hot = one_hot(iota((RADIX, hot_total), 0) == (hot & (RADIX - 1)))
    high_hot = one_hot(iota((high_rows, hot_total), 0) == (hot // RADIX))
    marks = lax.dot_general(low_hot, high_hot, ROWS_DOT, preferred_element_type=F32).astype(BF16)
    low_iota = iota((RADIX, q_rows), 0)
    high_iota = iota((high_rows, q_rows), 0)

    def lookup(tables, ids):
        hots = jnp.concatenate([one_hot(high_iota == (i // RADIX)) for i in ids], axis=1)
        found = [jnp.dot(t, hots, preferred_element_type=F32) for t in tables]
        masks = [low_iota == (i & (RADIX - 1)) for i in ids]
        return [
            [pick_rows(m, f[:, n * q_rows : (n + 1) * q_rows]) for n, m in enumerate(masks)]
            for f in found
        ]

    def check(j, carry):
        start = pl.multiple_of(j * 8, 8)
        rows = cand_t[pl.ds(start, 8), :]
        hits = lookup([marks], [rows[n : n + 1, :] for n in range(8)])[0]
        hit_t[pl.ds(start, 8), :] = jnp.concatenate(hits, axis=0)
        return carry

    lax.fori_loop(0, cand_count // 8, check, 0)
    cold = hit_t[...] < 0.5
    earlier = one_hot(iota((cand_count, cand_count), 0) > iota((cand_count, cand_count), 1))
    order = jnp.dot(earlier, one_hot(cold), preferred_element_type=F32).astype(jnp.int32)
    sel = jnp.where(cold, order, -1)
    sel_ref[...] = sel
    cand = cand_t[...]
    ids = [pick_rows(sel == r, cand) for r in range(COLD)]
    loc = jnp.concatenate([loc_ref[pl.ds(0, high_rows, stride=2), :], loc_ref[pl.ds(1, high_rows, stride=2), :]], axis=1)
    high_table = jnp.transpose((loc // RADIX).astype(F32)).astype(BF16)
    low_table = jnp.transpose((loc & (RADIX - 1)).astype(F32)).astype(BF16)
    high_part, low_part = lookup([high_table, low_table], ids)
    before = one_hot(iota((q_rows, q_rows), 0) < iota((q_rows, q_rows), 1))
    owner_iota = iota((groups, q_rows), 0)
    slot_iota = iota((LANES, q_rows), 0)
    query = iota((1, q_rows), 1).astype(F32)
    base = jnp.zeros((groups, 1), F32)
    owners, ranks, owner_hots, low_vals, high_vals, query_vals = [], [], [], [], [], []
    for r in range(COLD):
        row = high_part[r].astype(jnp.int32) * RADIX + low_part[r].astype(jnp.int32)
        owner = row // per_owner
        local = row & (per_owner - 1)
        owner_hot = one_hot(owner_iota == owner, F32)
        count = jnp.dot(owner_hot.astype(BF16), before, preferred_element_type=F32) + base
        rank = jnp.sum(owner_hot * count, axis=0, keepdims=True).astype(jnp.int32)
        base = base + jnp.sum(owner_hot, axis=1, keepdims=True)
        at_slot = slot_iota == rank
        owners.append(owner)
        ranks.append(rank)
        owner_hots.append(owner_hot.astype(BF16))
        low_vals.append(jnp.where(at_slot, (local & (RADIX - 1)).astype(F32), 0.0).astype(BF16))
        high_vals.append(jnp.where(at_slot, (local // RADIX + RADIX // 2).astype(F32), 0.0).astype(BF16))
        query_vals.append(jnp.where(at_slot, query, 0.0).astype(BF16))
    owner_all = jnp.concatenate(owner_hots, axis=1)

    def spread(vals):
        got = lax.dot_general(owner_all, jnp.concatenate(vals, axis=1), ROWS_DOT, preferred_element_type=F32)
        return got.astype(jnp.int32)

    low_got, high_got, query_got = spread(low_vals), spread(high_vals), spread(query_vals)
    packed = low_got + RADIX * (high_got - RADIX // 2) + per_owner * query_got
    req_ref[...] = jnp.where(high_got > 0, packed, -1)
    place_ref[...] = jnp.concatenate(owners + ranks, axis=0)


def prep_kernel(per_owner, spot_ref, q_ref, hot_ref, loc_ref, slab_ref, out_ref, col_scr):
    hot_each = out_ref.shape[0] - q_ref.shape[0]
    high_rows = loc_ref.shape[0]
    ids = hot_ref[pl.ds(spot_ref[0] * hot_each // LANES, 1), :]
    high_hot = one_hot(iota((high_rows, LANES), 0) == (ids // LANES))
    low_mask = iota((LANES, LANES), 0) == (ids & (LANES - 1))
    loc = loc_ref[...]
    high = jnp.transpose((loc // RADIX).astype(F32)).astype(BF16)
    low = jnp.transpose((loc & (RADIX - 1)).astype(F32)).astype(BF16)
    high = pick_rows(low_mask, jnp.dot(high, high_hot, preferred_element_type=F32))
    low = pick_rows(low_mask, jnp.dot(low, high_hot, preferred_element_type=F32))
    local = high * RADIX + low - (spot_ref[0] * per_owner).astype(F32)
    col_scr[...] = jnp.transpose(jnp.broadcast_to(local, (LANES, LANES)))
    start = pl.multiple_of(spot_ref[0] * hot_each % LANES, hot_each)
    cols = jnp.concatenate([col_scr[pl.ds(start, hot_each), :]] * (per_owner // LANES), axis=1)
    picks = one_hot(iota((hot_each, per_owner), 1).astype(F32) == cols)
    rows = jnp.dot(picks, slab_ref[...], preferred_element_type=F32).astype(BF16)
    out_ref[0 : q_ref.shape[0], :] = q_ref[...]
    out_ref[q_ref.shape[0] :, :] = rows


def fetch_kernel(capacity, asked_ref, slab_ref, out_ref):
    groups = asked_ref.shape[0]
    per_owner = slab_ref.shape[0]
    asked = jnp.maximum(asked_ref[...], 0)
    cols = jnp.transpose((asked & (per_owner - 1)).astype(F32))
    lane = iota((capacity, per_owner), 1).astype(F32)
    picks = [
        one_hot(lane == jnp.broadcast_to(cols[0:capacity, n : n + 1], (capacity, per_owner)), F32)
        for n in range(groups)
    ]
    got = jnp.dot(jnp.concatenate(picks, axis=0).astype(BF16), slab_ref[...], preferred_element_type=F32)
    out_ref[...] = got.astype(BF16)


def cold_kernel(scale, capacity, q_ref, found_ref, place_ref, cold_ref):
    q_rows = q_ref.shape[0]
    q = q_ref[...]
    place = place_ref[...]
    dests = [place[r : r + 1] * capacity + place[COLD + r : COLD + r + 1] for r in range(COLD)]
    colds = [jnp.zeros((1, q_rows), F32) for _ in range(COLD)]
    chunk = 256
    for j in range(found_ref.shape[0] // chunk):
        rows = found_ref[j * chunk : (j + 1) * chunk, :]
        got = scale * lax.dot_general(rows, q, ROWS_DOT, preferred_element_type=F32)
        ids = iota((chunk, q_rows), 0) + j * chunk
        for r in range(COLD):
            colds[r] = colds[r] + pick_rows(ids == dests[r], got)
    cold_ref[...] = jnp.concatenate(colds, axis=0)


def count_kernel(cand_t, teacher_ref, hot_ref, sel_ref, count_ref, target_ref, misc_ref, soft_t):
    cand_count, q_rows = cand_t.shape
    teacher = teacher_ref[...]
    shifted = teacher - jnp.max(teacher, axis=0, keepdims=True)
    log_target = shifted - jnp.log(jnp.sum(jnp.exp(shifted), axis=0, keepdims=True))
    target = jnp.exp(log_target)
    soft_t[...] = target
    sel = sel_ref[...]
    entropy = jnp.sum(target * log_target, axis=0, keepdims=True)
    rows = [pick_rows(sel == r, target) for r in range(COLD)]
    misc_ref[...] = jnp.concatenate(rows + [jnp.broadcast_to(entropy, (8, q_rows))], axis=0)
    hot_cols = jnp.transpose(hot_ref[...])
    for a in range(hot_ref.shape[0]):
        column = jnp.broadcast_to(hot_cols[:, a : a + 1], (LANES, q_rows))

        def add(k, carry):
            count, total = carry
            match = column == cand_t[pl.ds(k, 1), :]
            count = count + jnp.where(match, 1.0, 0.0)
            total = total + jnp.where(match, soft_t[pl.ds(k, 1), :], 0.0)
            return count, total

        start = (jnp.ones((LANES, q_rows), F32), jnp.zeros((LANES, q_rows), F32))
        count, total = lax.fori_loop(0, cand_count, add, start, unroll=4)
        count_ref[a * LANES : (a + 1) * LANES, :] = count
        target_ref[a * LANES : (a + 1) * LANES, :] = total


def score_kernel(scale, q_ref, hot_ref, cold_ref, count_ref, target_ref, place_ref, misc_ref, loss_ref, pay_ref, weight_ref, hot_scr, slot_scr):
    groups, hot_each, feat = hot_ref.shape
    q_rows = q_ref.shape[0]
    q = q_ref[...]
    top = jnp.max(cold_ref[...], axis=0, keepdims=True)
    step = 8
    for j in range(groups // step):
        size = step * hot_each
        rows = hot_ref[j * step : (j + 1) * step].reshape(size, feat)
        got = scale * lax.dot_general(rows, q, ROWS_DOT, preferred_element_type=F32)
        hot_scr[j * size : (j + 1) * size, :] = got
        top = jnp.maximum(top, jnp.max(got, axis=0, keepdims=True))
    cold = cold_ref[...]
    place = place_ref[...]
    total = jnp.sum(jnp.exp(cold - top), axis=0, keepdims=True)
    hot_dot = jnp.zeros((1, q_rows), F32)
    for j in range(groups // 8):
        part = slice(j * 8 * hot_each, (j + 1) * 8 * hot_each)
        hot = hot_scr[part, :]
        total = total + jnp.sum(count_ref[part, :] * jnp.exp(hot - top), axis=0, keepdims=True)
        hot_dot = hot_dot + jnp.sum(target_ref[part, :] * hot, axis=0, keepdims=True)
    log_total = top + jnp.log(total)
    cold_target = misc_ref[0:COLD, :]
    entropy = misc_ref[COLD : COLD + 1, :]
    loss_ref[...] = entropy - hot_dot - jnp.sum(cold_target * cold, axis=0, keepdims=True) + log_total
    weight = (jnp.exp(cold - log_total) - cold_target).astype(BF16).astype(F32)
    weight_ref[...] = weight
    owner_iota = iota((groups, q_rows), 0)
    slot_iota = iota((LANES, q_rows), 0)
    owner_all = jnp.concatenate([one_hot(owner_iota == place[r : r + 1]) for r in range(COLD)], axis=1)
    slot_all = jnp.concatenate(
        [
            jnp.where(slot_iota == place[COLD + r : COLD + r + 1], weight[r : r + 1], 0.0).astype(BF16)
            for r in range(COLD)
        ],
        axis=1,
    )
    slot_scr[...] = lax.dot_general(owner_all, slot_all, ROWS_DOT, preferred_element_type=F32)
    for g in range(groups):
        part = slice(g * hot_each, (g + 1) * hot_each)
        coef = count_ref[part, :] * jnp.exp(hot_scr[part, :] - log_total) - target_ref[part, :]
        slot_row = jnp.broadcast_to(slot_scr[g : g + 1, :], (8, q_rows))
        pay_ref[g] = jnp.concatenate([coef, slot_row], axis=0).astype(BF16)


def query_kernel(scale, capacity, hot_ref, pay_ref, found_ref, weight_ref, place_ref, out_ref):
    groups, hot_each, feat = hot_ref.shape
    q_rows = out_ref.shape[0]
    acc = jnp.zeros(out_ref.shape, F32)
    step = 8
    first = (((0,), (0,)), ((), ()))
    for j in range(groups // step):
        rows = hot_ref[j * step : (j + 1) * step].reshape(step * hot_each, feat)
        coef = jnp.concatenate([pay_ref[j * step + n, 0:hot_each, :] for n in range(step)], axis=0)
        acc = acc + lax.dot_general(coef, rows, first, preferred_element_type=F32)
    chunk = 256
    place = place_ref[...]
    weight = weight_ref[...]
    dests = [place[r : r + 1] * capacity + place[COLD + r : COLD + r + 1] for r in range(COLD)]
    for j in range(found_ref.shape[0] // chunk):
        ids = iota((chunk, q_rows), 0) + j * chunk
        made = jnp.zeros((chunk, q_rows), F32)
        for r in range(COLD):
            made = jnp.where(ids == dests[r], weight[r : r + 1], made)
        rows = found_ref[j * chunk : (j + 1) * chunk, :]
        acc = acc + lax.dot_general(made.astype(BF16), rows, first, preferred_element_type=F32)
    out_ref[...] = scale * acc


def slab_kernel(scale, capacity, hot_each, spot_ref, pay_ref, row_ref, loc_ref, *refs):
    outs, terms = refs[:-1], refs[-1]
    step = pl.program_id(0)
    groups = pay_ref.shape[0]
    feat = terms.shape[1]
    sent = jnp.concatenate([pay_ref[n, hot_each : hot_each + 8, :].astype(F32)[0:1] for n in range(groups)], axis=0)
    cols = scale * jnp.transpose(sent)
    col = jnp.concatenate(
        [jnp.broadcast_to(cols[0:capacity, n : n + 1], (capacity, LANES)) for n in range(groups)], axis=0
    )
    size = groups * capacity
    wide = jnp.concatenate([col] * (feat // LANES), axis=1)
    made = (wide * row_ref[...].astype(F32)).astype(BF16)
    terms[pl.ds(pl.multiple_of(step * size, size), size), :] = made

    @pl.when(step == pl.num_programs(0) - 1)
    def _():
        loc = loc_ref[...]
        rows = outs[0].shape[0]
        ids = iota((rows, loc.shape[1]), 0)
        for d in range(0, len(outs), 2):
            starts = [(spot_ref[1] + e) % len(outs) * rows for e in (d, d + 1)]
            at = jnp.concatenate([one_hot(ids + start == loc) for start in starts], axis=0)
            got = jnp.dot(at, terms[...], preferred_element_type=F32)
            outs[d][...] = got[:rows].astype(outs[d].dtype)
            outs[d + 1][...] = got[rows:].astype(outs[d + 1].dtype)


def hot_sum_kernel(scale, pay_ref, query_ref, out_ref):
    step = pl.program_id(0)
    groups = pay_ref.shape[0]
    hot_each = out_ref.shape[0]

    @pl.when(step == 0)
    def _():
        out_ref[...] = jnp.zeros_like(out_ref)

    acc = out_ref[...]
    for n in range(0, groups, 2):
        left = jnp.concatenate([pay_ref[n, 0:hot_each, :], pay_ref[n + 1, 0:hot_each, :]], axis=1)
        right = jnp.concatenate([query_ref[n], query_ref[n + 1]], axis=0)
        acc = acc + scale * jnp.dot(left, right, preferred_element_type=F32)
    out_ref[...] = acc


def finish_kernel(reps, spot_ref, hot_loc_ref, *refs):
    hots, parts, out_ref = refs[:reps], refs[reps:-1], refs[-1]
    rows = out_ref.shape[0]
    full = hots[0][...]
    for hot in hots[1:]:
        full = full + hot[...]
    high = full.astype(BF16)
    rest = full - high.astype(F32)
    mid = rest.astype(BF16)
    low = (rest - mid.astype(F32)).astype(BF16)
    pieces = jnp.concatenate([high, mid, low, jnp.zeros_like(low)], axis=0)
    loc = hot_loc_ref[...]
    at = one_hot(iota((rows, loc.shape[1]), 0) + spot_ref[1] * rows == loc)
    total = jnp.dot(at, pieces, preferred_element_type=F32)
    for part in parts:
        total = total + part[...].astype(F32)
    out_ref[...] = total


def shards(queries, teacher, slab, candidates, hot_ids, location):
    groups = lax.axis_size("corpus")
    reps = lax.axis_size("rep")
    corpus_idx = lax.axis_index("corpus")
    q_rows, feat = queries.shape
    per_owner = slab.shape[0]
    hot_total = hot_ids.shape[0]
    hot_each = hot_total // groups
    cand_count = candidates.shape[1]
    capacity = q_rows * COLD * 3 // (2 * groups)
    scale = 2.0 / math.sqrt(feat)
    rep_idx = lax.axis_index("rep")
    spot = jnp.stack([corpus_idx, rep_idx]).astype(jnp.int32)
    loc_table = location.reshape(-1, LANES)
    hot_table = hot_ids.reshape(-1, LANES)
    sent_rows = pl.pallas_call(
        functools.partial(prep_kernel, per_owner),
        out_shape=jax.ShapeDtypeStruct((q_rows + hot_each, feat), BF16),
        in_specs=[SMEM_SPEC] + [VMEM_SPEC] * 4,
        out_specs=VMEM_SPEC,
        scratch_shapes=[pltpu.VMEM((LANES, LANES), F32)],
        name="prep",
    )(spot, queries, hot_table, loc_table, slab)
    cand_t, sent_rows = lax.optimization_barrier((candidates.T, sent_rows))
    gathered = lax.all_gather(sent_rows, "corpus", axis=0, tiled=False)
    req, place, sel = pl.pallas_call(
        functools.partial(request_kernel, per_owner, groups),
        out_shape=(
            jax.ShapeDtypeStruct((groups, LANES), jnp.int32),
            jax.ShapeDtypeStruct((2 * COLD, q_rows), jnp.int32),
            jax.ShapeDtypeStruct((cand_count, q_rows), jnp.int32),
        ),
        in_specs=[VMEM_SPEC] * 3,
        out_specs=(VMEM_SPEC,) * 3,
        scratch_shapes=[pltpu.VMEM((cand_count, q_rows), F32)],
        name="request",
    )(cand_t, hot_ids.reshape(1, hot_total), loc_table)
    asked = lax.all_to_all(req.reshape(groups, 1, LANES), "corpus", split_axis=0, concat_axis=0, tiled=True)
    asked = asked.reshape(groups, LANES)
    slots = groups * capacity
    parts = 4
    wanted = pl.pallas_call(
        functools.partial(fetch_kernel, capacity),
        grid=(parts,),
        out_shape=jax.ShapeDtypeStruct((slots, feat), BF16),
        in_specs=[pl.BlockSpec((groups // parts, LANES), lambda i: (i, 0)), pl.BlockSpec((per_owner, feat), lambda i: (0, 0))],
        out_specs=pl.BlockSpec((slots // parts, feat), lambda i: (i, 0)),
        name="fetch",
    )(asked, slab)
    found = lax.all_to_all(wanted.reshape(groups, capacity, feat), "corpus", split_axis=0, concat_axis=0, tiled=True)
    found = found.reshape(groups * capacity, feat)
    count, target, misc = pl.pallas_call(
        count_kernel,
        out_shape=(
            jax.ShapeDtypeStruct((hot_total, q_rows), F32),
            jax.ShapeDtypeStruct((hot_total, q_rows), F32),
            jax.ShapeDtypeStruct((2 * COLD, q_rows), F32),
        ),
        in_specs=[VMEM_SPEC] * 4,
        out_specs=(VMEM_SPEC,) * 3,
        scratch_shapes=[pltpu.VMEM((cand_count, q_rows), F32)],
        cost_estimate=pl.CostEstimate(flops=80_000_000, bytes_accessed=3_000_000, transcendentals=10_000),
        name="count",
    )(cand_t, teacher.T, hot_table, sel)
    hot_block = pl.BlockSpec((groups, hot_each, feat), lambda i: (0, q_rows // hot_each, 0))

    def whole(shape):
        return pl.BlockSpec(shape, lambda i: (0,) * len(shape))

    pay_rows = hot_each + 8
    cold = pl.pallas_call(
        functools.partial(cold_kernel, scale, capacity),
        out_shape=jax.ShapeDtypeStruct((COLD, q_rows), F32),
        in_specs=[VMEM_SPEC] * 3,
        out_specs=VMEM_SPEC,
        name="cold",
    )(queries, found, place)
    loss, pay, weight = pl.pallas_call(
        functools.partial(score_kernel, scale),
        grid=(1,),
        out_shape=(
            jax.ShapeDtypeStruct((1, q_rows), F32),
            jax.ShapeDtypeStruct((groups, pay_rows, q_rows), BF16),
            jax.ShapeDtypeStruct((COLD, q_rows), F32),
        ),
        in_specs=[
            whole((q_rows, feat)),
            hot_block,
            whole((COLD, q_rows)),
            whole((hot_total, q_rows)),
            whole((hot_total, q_rows)),
            whole((2 * COLD, q_rows)),
            whole((2 * COLD, q_rows)),
        ],
        out_specs=(whole((1, q_rows)), whole((groups, pay_rows, q_rows)), whole((COLD, q_rows))),
        scratch_shapes=[
            pltpu.VMEM((hot_total, q_rows), F32),
            pltpu.VMEM((groups, q_rows), F32),
        ],
        name="score",
    )(queries, gathered, cold, count, target, place, misc)
    got = lax.all_to_all(pay, "corpus", split_axis=0, concat_axis=0, tiled=True)
    query_grad = pl.pallas_call(
        functools.partial(query_kernel, scale, capacity),
        grid=(1,),
        out_shape=jax.ShapeDtypeStruct((q_rows, feat), F32),
        in_specs=[hot_block, whole((groups, pay_rows, q_rows)), whole((slots, feat)), whole((COLD, q_rows)), whole((2 * COLD, q_rows))],
        out_specs=whole((q_rows, feat)),
        cost_estimate=pl.CostEstimate(flops=700_000_000, bytes_accessed=7_000_000, transcendentals=0),
        name="query_grad",
    )(gathered, pay, found, weight, place)
    padded = asked[:, :capacity]
    source = jnp.arange(groups, dtype=jnp.int32)[:, None] * (q_rows + hot_each)
    query_rows = gathered.reshape(-1, feat)[(source + jnp.maximum(padded, 0) // per_owner).reshape(-1)]
    local = jnp.where(padded >= 0, padded & (per_owner - 1), -1).reshape(1, -1)
    mine = lax.dynamic_slice_in_dim(hot_ids, corpus_idx * hot_each, hot_each)
    own_hot = location[mine] - corpus_idx * per_owner
    tail = jnp.full((LANES - 3 * hot_each,), -1, jnp.int32)
    hot_loc = jnp.concatenate([own_hot, own_hot, own_hot, tail])[None, :]
    step = 16
    quarter = (per_owner // reps, feat)
    quarters = pl.pallas_call(
        functools.partial(slab_kernel, scale, capacity, hot_each),
        grid=(groups // step,),
        out_shape=tuple(jax.ShapeDtypeStruct(quarter, F32 if d == 0 else BF16) for d in range(reps)),
        in_specs=[
            SMEM_SPEC,
            pl.BlockSpec((step, pay_rows, q_rows), lambda i: (i, 0, 0)),
            pl.BlockSpec((step * capacity, feat), lambda i: (i, 0)),
            whole((1, slots)),
        ],
        out_specs=tuple(whole(quarter) for _ in range(reps)),
        scratch_shapes=[pltpu.VMEM((slots, feat), BF16)],
        name="slab_grad",
    )(spot, got, query_rows, local)

    def turn(array, d):
        return lax.ppermute(array, "rep", [(r, (r + d) % reps) for r in range(reps)])

    received = [turn(quarters[d], d) for d in (2, 1, 3)]
    hot_sum = pl.pallas_call(
        functools.partial(hot_sum_kernel, scale),
        grid=(groups // step,),
        out_shape=jax.ShapeDtypeStruct((hot_each, feat), F32),
        in_specs=[
            pl.BlockSpec((step, pay_rows, q_rows), lambda i: (i, 0, 0)),
            pl.BlockSpec((step, q_rows, feat), lambda i: (i, 0, 0)),
        ],
        out_specs=whole((hot_each, feat)),
        cost_estimate=pl.CostEstimate(flops=3_000_000_000, bytes_accessed=13_000_000, transcendentals=0),
        name="hot_sum",
    )(got, gathered)
    hots = [hot_sum] + [turn(hot_sum, d) for d in range(1, reps)]
    slab_grad = pl.pallas_call(
        functools.partial(finish_kernel, reps),
        out_shape=jax.ShapeDtypeStruct(quarter, F32),
        in_specs=[SMEM_SPEC] + [VMEM_SPEC] * (2 * reps + 1),
        out_specs=VMEM_SPEC,
        name="finish",
    )(spot, hot_loc, *hots, quarters[0], *received)
    return (loss.reshape(q_rows), query_grad, slab_grad)


def solution(mesh):
    return jax.shard_map(
        shards,
        mesh=mesh,
        in_specs=(
            P(("corpus", "rep"), None),
            P(("corpus", "rep"), None),
            P("corpus", None),
            P(("corpus", "rep"), None),
            P(),
            P(),
        ),
        out_specs=(P(("corpus", "rep")), P(("corpus", "rep"), None), P(("corpus", "rep"), None)),
        check_vma=False,
    )
```

profile of v0, /device:TPU:6, one launch (start us, length us, event | category | flops | bytes accessed | tf_op | source)
XLA Modules:
  0.0 228.1 jit_solution(5245814505893453081)
XLA Ops:
  7.9 3.2 %prep.1 = bf16[160,768]{1,0:T(8,128)(2,1)} custom-call(s32[2]{0:T(128)} %pad_add_fusion.spot_ref, bf16[128,768]{1,0:T(8,128)(2,1)} %q_ref.5, s32[16,128]{1,0:T(8,128)} %bitcast.27, s32[512,128]{1,0:T(8,128)} %bitcast.23, bf16[1024,768]{1,0:T(8,128)(2,1)} %slab_ref.3), custom_call_target="tpu_custom_call" | custom-call | tf_op jit(solution)/shard_map/prep/pallas_call | solution.py:333
  11.1 6.2 %request.1 = (s32[64,128]{1,0:T(8,128)}, s32[16,128]{1,0:T(8,128)}, s32[64,128]{1,0:T(8,128)}) custom-call(s32[64,128]{1,0:T(8,128)} %bitcast.30, s32[1,2048]{1,0:T(1,128)} %bitcast.28, s32[512,128]{1,0:T(8,128)} %bitcast.24), custom_call_target="tpu_custom_call" | custom-call | tf_op jit(solution)/shard_map/request/pallas_call | solution.py:343
  17.3 19.7 %all_to_all.15 = s32[64,1,128]{2,1,0:T(1,128)} all-to-all(s32[64,1,128]{2,1,0:T(1,128)} %bitcast.32), channel_id=1, replica_groups=mesh['corpus'=64,'rep'=4] {'corpus'}, dimensions={0} | all-to-all | bytes 65536 | tf_op jit(solution)/shard_map/all_to_all | solution.py:355
  37.0 5.9 %fetch.1 = bf16[1536,768]{1,0:T(8,128)(2,1)} custom-call(s32[64,128]{1,0:T(8,128)} %bitcast.25, bf16[1024,768]{1,0:T(8,128)(2,1)} %slab_ref.3), custom_call_target="tpu_custom_call" | custom-call | tf_op jit(solution)/shard_map/fetch/pallas_call | solution.py:359
  42.9 6.6 %all-to-all-start.1 = ((bf16[64,24,768]{2,1,0:T(8,128)(2,1)}), bf16[64,24,768]{2,1,0:T(8,128)(2,1)S(1)}, u32[]{:S(2)}, u32[]{:S(2)}) async-start(bf16[64,24,768]{2,1,0:T(8,128)(2,1)} %bitcast.22), calls=%async_computation.1 | async-start | bytes 4718592 | tf_op jit(solution)/shard_map/all_to_all | solution.py:367
  49.5 18.4 %count.1 = (f32[2048,128]{1,0:T(8,128)}, f32[2048,128]{1,0:T(8,128)}, f32[16,128]{1,0:T(8,128)}) custom-call(s32[64,128]{1,0:T(8,128)} %bitcast.31, f32[64,128]{1,0:T(8,128)} %bitcast.33, s32[16,128]{1,0:T(8,128)} %bitcast.29, s32[64,128]{1,0:T(8,128)} %get-tuple-element.22.sel_ref), custom_call_target="tpu_custom_call" | custom-call | flops 80000000 | bytes 3000000 | tf_op jit(solution)/shard_map/count/pallas_call | solution.py:369
  68.0 53.1 %all-to-all-done.1 = bf16[64,24,768]{2,1,0:T(8,128)(2,1)S(1)} async-done(((bf16[64,24,768]{2,1,0:T(8,128)(2,1)}), bf16[64,24,768]{2,1,0:T(8,128)(2,1)S(1)}, u32[]{:S(2)}, u32[]{:S(2)}) %all-to-all-start.1) | async-done | bytes 2359328 | tf_op jit(solution)/shard_map/all_to_all | solution.py:367
  121.0 1.4 copy-done
  122.4 3.5 %cold.1.cold_ref = f32[8,128]{1,0:T(8,128)} custom-call(bf16[128,768]{1,0:T(8,128)(2,1)} %q_ref.5, bf16[1536,768]{1,0:T(8,128)(2,1)} %bitcast.20, s32[16,128]{1,0:T(8,128)} %get-tuple-element.21.place_ref), custom_call_target="tpu_custom_call" | custom-call | tf_op jit(solution)/shard_map/cold/pallas_call | solution.py:388
  125.9 17.0 %all-gather.3.cloned.1.call-done = bf16[10240,768]{1,0:T(8,128)(2,1)} async-done(((bf16[160,768]{1,0:T(8,128)(2,1)}), bf16[10240,768]{1,0:T(8,128)(2,1)}) %all-gather.3.cloned.1.call-update) | async-done | bytes 15728656 | tf_op jit(solution)/shard_map/all_gather | solution.py:342
  142.9 5.5 %score.1 = (f32[1,128]{1,0:T(1,128)}, bf16[64,40,128]{2,1,0:T(8,128)(2,1)}, f32[8,128]{1,0:T(8,128)}) custom-call(bf16[128,768]{1,0:T(8,128)(2,1)} %q_ref.5, bf16[64,160,768]{2,1,0:T(8,128)(2,1)} %bitcast.17, f32[8,128]{1,0:T(8,128)} %cold.1.cold_ref, f32[2048,128]{1,0:T(8,128)} %get-tuple-element.23.count_ref, f32[2048,128]{1,0:T(8,128)} %get-tuple-element.24.target_ref, ...), custom_call_target="tpu_custom_call" | custom-call | tf_op jit(solution)/shard_map/score/pallas_call | solution.py:395
  148.4 8.1 %all-to-all-start.2 = ((bf16[64,40,128]{2,1,0:T(8,128)(2,1)}), bf16[64,40,128]{2,1,0:T(8,128)(2,1)S(1)}, u32[]{:S(2)}, u32[]{:S(2)}) async-start(bf16[64,40,128]{2,1,0:T(8,128)(2,1)} %get-tuple-element.27.pay_ref), calls=%async_computation.2 | async-start | bytes 1310720 | tf_op jit(solution)/shard_map/all_to_all | solution.py:419
  158.9 14.2 %gather_fusion.1 = bf16[1536,768]{1,0:T(8,128)(2,1)} fusion(bf16[10240,768]{1,0:T(8,128)(2,1)} %all-gather.3.cloned.1.call-done, s32[2048]{0:T(1024)S(1)} %pad_clamp_fusion), kind=kCustom, calls=%fused_computation.1 | custom fusion | bytes 4724736 | tf_op jit(solution)/shard_map/gather | solution.py:431
  173.1 2.7 %all-to-all-done.2.pay_ref = bf16[64,40,128]{2,1,0:T(8,128)(2,1)S(1)} async-done(((bf16[64,40,128]{2,1,0:T(8,128)(2,1)}), bf16[64,40,128]{2,1,0:T(8,128)(2,1)S(1)}, u32[]{:S(2)}, u32[]{:S(2)}) %all-to-all-start.2) | async-done | bytes 655392 | tf_op jit(solution)/shard_map/all_to_all | solution.py:419
  176.6 7.1 %hot_sum.1.refs_0_ = f32[32,768]{1,0:T(8,128)} custom-call(bf16[64,40,128]{2,1,0:T(8,128)(2,1)} %copy-done.1, bf16[64,160,768]{2,1,0:T(8,128)(2,1)} %bitcast.18), custom_call_target="tpu_custom_call" | custom-call | flops 3000000000 | bytes 13000000 | tf_op jit(solution)/shard_map/hot_sum/pallas_call | solution.py:458
  183.7 1.6 collective-permute-start
  185.3 7.1 %slab_grad.1 = (f32[256,768]{1,0:T(8,128)}, bf16[256,768]{1,0:T(8,128)(2,1)}, bf16[256,768]{1,0:T(8,128)(2,1)}, bf16[256,768]{1,0:T(8,128)(2,1)}) custom-call(s32[2]{0:T(128)} %pad_add_fusion.spot_ref, bf16[64,40,128]{2,1,0:T(8,128)(2,1)} %copy-done.1, bf16[1536,768]{1,0:T(8,128)(2,1)} %gather_fusion.1, s32[1,1536]{1,0:T(1,128)} %reshape.82.loc_ref), custom_call_target="tpu_custom_call" | custom-call | tf_op jit(solution)/shard_map/slab_grad/pallas_call | solution.py:439
  192.4 2.8 %collective-permute-start.3 = (bf16[256,768]{1,0:T(8,128)(2,1)}, bf16[256,768]{1,0:T(8,128)(2,1)S(1)}, u32[]{:S(2)}, u32[]{:S(2)}) collective-permute-start(bf16[256,768]{1,0:T(8,128)(2,1)} %get-tuple-element.30), channel_id=1, source_target_pairs={{0,2},{1,3},{2,0},{3,1},{4,6},{5,7},{6,4},{7,5},{8,10},{9,11},{10,... | collective-permute-start | bytes 1179656 | tf_op jit(solution)/shard_map/ppermute | solution.py:455
  195.2 3.2 %collective-permute-start.5 = (bf16[256,768]{1,0:T(8,128)(2,1)}, bf16[256,768]{1,0:T(8,128)(2,1)S(1)}, u32[]{:S(2)}, u32[]{:S(2)}) collective-permute-start(bf16[256,768]{1,0:T(8,128)(2,1)} %get-tuple-element.32), channel_id=1, source_target_pairs={{0,3},{1,0},{2,1},{3,2},{4,7},{5,4},{6,5},{7,6},{8,11},{9,8},{10,9... | collective-permute-start | bytes 1179656 | tf_op jit(solution)/shard_map/ppermute | solution.py:455
  198.5 1.4 collective-permute-start.2
  200.6 4.6 %query_grad.1 = f32[128,768]{1,0:T(8,128)} custom-call(bf16[64,160,768]{2,1,0:T(8,128)(2,1)} %bitcast.19, bf16[64,40,128]{2,1,0:T(8,128)(2,1)} %get-tuple-element.27.pay_ref, bf16[1536,768]{1,0:T(8,128)(2,1)} %bitcast.21, f32[8,128]{1,0:T(8,128)} %get-tuple-element.28.weight_ref, s32[16,128]{1,0:T(8,128)} %get-tuple-element.21.place_ref), custom_call_target="tpu_custom_call" | custom-call | flops 700000000 | bytes 7000000 | tf_op jit(solution)/shard_map/query_grad/pallas_call | solution.py:420
  205.2 11.0 %collective-permute-done.1.refs_2_ = f32[32,768]{1,0:T(8,128)S(1)} collective-permute-done((f32[32,768]{1,0:T(8,128)S(1)}, f32[32,768]{1,0:T(8,128)S(1)}, u32[]{:S(2)}, u32[]{:S(2)}) %collective-permute-start.1) | collective-permute-done | bytes 98336 | tf_op jit(solution)/shard_map/ppermute | solution.py:455
  216.2 1.2 collective-permute-done.2.refs_3_
  218.4 2.8 %finish.1 = f32[256,768]{1,0:T(8,128)} custom-call(s32[2]{0:T(128)} %pad_add_fusion.spot_ref, s32[1,128]{1,0:T(1,128)} %add_bitcast_fusion.hot_loc_ref, f32[32,768]{1,0:T(8,128)} %hot_sum.1.refs_0_, f32[32,768]{1,0:T(8,128)} %copy-done.8, f32[32,768]{1,0:T(8,128)} %copy-done.9, f32[32,768]{1,0:T(8,128)} %copy-done.10, f32[256,768]{1,0:T(8,128)} %get-tuple-element.29.refs_4_, ...), custom_call_target="tpu_custom_call" | custom-call | tf_op jit(solution)/shard_map/finish/pallas_call | solution.py:471
  (42 shorter events, 5.6 us)
Async XLA Ops:
  7.2 135.7 %all-gather.3.cloned.1.call-start = ((), (), s32[]{:S(2)}) async-start(), calls=%async_computation.3 | async-start | bytes 15974400 | tf_op jit(solution)/shard_map/all_gather | solution.py:342
  42.9 78.1 %all-to-all-start.1 = ((bf16[64,24,768]{2,1,0:T(8,128)(2,1)}), bf16[64,24,768]{2,1,0:T(8,128)(2,1)S(1)}, u32[]{:S(2)}, u32[]{:S(2)}) async-start(bf16[64,24,768]{2,1,0:T(8,128)(2,1)} %bitcast.22), calls=%async_computation.1 | async-start | bytes 4718592 | tf_op jit(solution)/shard_map/all_to_all | solution.py:367
  121.0 1.4 copy-start
  142.9 14.4 %copy-start.2 = (s32[65536]{0:T(1024)S(1)}, s32[65536]{0:T(1024)}, u32[]{:S(2)}) copy-start(s32[65536]{0:T(1024)} %param.11) | copy-start | bytes 786436
  142.9 15.1 %copy-start.7 = (s32[64,1,128]{2,1,0:T(1,128)S(1)}, s32[64,1,128]{2,1,0:T(1,128)}, u32[]{:S(2)}) copy-start(s32[64,1,128]{2,1,0:T(1,128)} %all_to_all.15) | copy-start | bytes 98308
  148.4 27.4 %all-to-all-start.2 = ((bf16[64,40,128]{2,1,0:T(8,128)(2,1)}), bf16[64,40,128]{2,1,0:T(8,128)(2,1)S(1)}, u32[]{:S(2)}, u32[]{:S(2)}) async-start(bf16[64,40,128]{2,1,0:T(8,128)(2,1)} %get-tuple-element.27.pay_ref), calls=%async_computation.2 | async-start | bytes 1310720 | tf_op jit(solution)/shard_map/all_to_all | solution.py:419
  175.8 0.8 copy-start.1
  183.7 14.7 %copy-start.3 = (f32[32,768]{1,0:T(8,128)S(1)}, f32[32,768]{1,0:T(8,128)}, u32[]{:S(2)}) copy-start(f32[32,768]{1,0:T(8,128)} %hot_sum.1.refs_0_) | copy-start | bytes 294916
  183.7 14.8 %collective-permute-start = (f32[32,768]{1,0:T(8,128)}, f32[32,768]{1,0:T(8,128)S(1)}, u32[]{:S(2)}, u32[]{:S(2)}) collective-permute-start(f32[32,768]{1,0:T(8,128)} %hot_sum.1.refs_0_), channel_id=1, source_target_pairs={{0,1},{1,2},{2,3},{3,0},{4,5},{5,6},{6,7},{7,4},{8,9},{9,10},{10,1... | collective-permute-start | bytes 294920 | tf_op jit(solution)/shard_map/ppermute | solution.py:455
  192.4 25.0 %collective-permute-start.3 = (bf16[256,768]{1,0:T(8,128)(2,1)}, bf16[256,768]{1,0:T(8,128)(2,1)S(1)}, u32[]{:S(2)}, u32[]{:S(2)}) collective-permute-start(bf16[256,768]{1,0:T(8,128)(2,1)} %get-tuple-element.30), channel_id=1, source_target_pairs={{0,2},{1,3},{2,0},{3,1},{4,6},{5,7},{6,4},{7,5},{8,10},{9,11},{10,... | collective-permute-start | bytes 1179656 | tf_op jit(solution)/shard_map/ppermute | solution.py:455
  195.2 22.2 %collective-permute-start.4 = (bf16[256,768]{1,0:T(8,128)(2,1)}, bf16[256,768]{1,0:T(8,128)(2,1)S(1)}, u32[]{:S(2)}, u32[]{:S(2)}) collective-permute-start(bf16[256,768]{1,0:T(8,128)(2,1)} %get-tuple-element.31), channel_id=1, source_target_pairs={{0,1},{1,2},{2,3},{3,0},{4,5},{5,6},{6,7},{7,4},{8,9},{9,10},{10,1... | collective-permute-start | bytes 1179656 | tf_op jit(solution)/shard_map/ppermute | solution.py:455
  195.2 22.2 %collective-permute-start.5 = (bf16[256,768]{1,0:T(8,128)(2,1)}, bf16[256,768]{1,0:T(8,128)(2,1)S(1)}, u32[]{:S(2)}, u32[]{:S(2)}) collective-permute-start(bf16[256,768]{1,0:T(8,128)(2,1)} %get-tuple-element.32), channel_id=1, source_target_pairs={{0,3},{1,0},{2,1},{3,2},{4,7},{5,4},{6,5},{7,6},{8,11},{9,8},{10,9... | collective-permute-start | bytes 1179656 | tf_op jit(solution)/shard_map/ppermute | solution.py:455
  198.5 17.7 %collective-permute-start.1 = (f32[32,768]{1,0:T(8,128)S(1)}, f32[32,768]{1,0:T(8,128)S(1)}, u32[]{:S(2)}, u32[]{:S(2)}) collective-permute-start(f32[32,768]{1,0:T(8,128)S(1)} %copy-done.3), channel_id=1, source_target_pairs={{0,2},{1,3},{2,0},{3,1},{4,6},{5,7},{6,4},{7,5},{8,10},{9,11},{10,... | collective-permute-start | bytes 294920 | tf_op jit(solution)/shard_map/ppermute | solution.py:455
  198.5 6.7 %copy-start.8 = (f32[32,768]{1,0:T(8,128)}, f32[32,768]{1,0:T(8,128)S(1)}, u32[]{:S(2)}) copy-start(f32[32,768]{1,0:T(8,128)S(1)} %collective-permute-done.refs_1_) | copy-start | bytes 294916
  198.5 18.9 %collective-permute-start.2 = (f32[32,768]{1,0:T(8,128)S(1)}, f32[32,768]{1,0:T(8,128)S(1)}, u32[]{:S(2)}, u32[]{:S(2)}) collective-permute-start(f32[32,768]{1,0:T(8,128)S(1)} %copy-done.3), channel_id=1, source_target_pairs={{0,3},{1,0},{2,1},{3,2},{4,7},{5,4},{6,5},{7,6},{8,11},{9,8},{10,9... | collective-permute-start | bytes 294920 | tf_op jit(solution)/shard_map/ppermute | solution.py:455
  216.2 1.2 copy-start.9
  217.4 0.7 copy-start.10
  217.4 0.8 copy-start.4
  217.4 0.9 copy-start.5
  217.4 1.0 copy-start.6
Sparse Core Ops, SparseCore 0:
  11.3 131.5 all-gather.2
where the time goes:
time: 230 us; the launch traced here: 228 us
  waiting for transfers between devices  85 us (37%)
  Pallas kernels  64.4 us (28%)
  starting transfers between devices  23.8 us (10%)
  blocking collectives  19.7 us (9%)
  local copies, waits for them, and re-layouts  18.9 us (8%)
  between operations  14.1 us (6%)
    all_to_all x1, waiting for transfers between devices, shards(): lax.all_to_all(wanted.reshape(groups, capacity, feat), 'corpus', split_ax...  53.1 us
    all_to_all x1, blocking collectives, shards(): lax.all_to_all(req.reshape(groups, 1, LANES), 'corpus', split_axis=0, con...  19.7 us
    pallas_call x1, Pallas kernels, shards(): pl.pallas_call(count_kernel, out_shape=(jax.ShapeDtypeStruct((hot_total,...  18.4 us
    all_gather x1, waiting for transfers between devices, shards(): gathered = lax.all_gather(sent_rows, 'corpus', axis=0, tiled=False)  17 us
    gather x1, local copies, waits for them, and re-layouts, shards(): gathered.reshape(-1, feat)  14.2 us
    ppermute x6, waiting for transfers between devices, turn(): lax.ppermute(array, 'rep', [(r, (r + d) % reps) for r in range(reps)])  12.2 us
    ppermute x6, starting transfers between devices, turn(): lax.ppermute(array, 'rep', [(r, (r + d) % reps) for r in range(reps)])  9.1 us
    all_to_all x1, starting transfers between devices, shards(): got = lax.all_to_all(pay, 'corpus', split_axis=0, concat_axis=0, tiled=True)  8.07 us
  transfers between devices with their start and end apart: 9, of which 5 were waited for; matrix products, arithmetic and copies ran while one was open for 8% of the time, Pallas kernels for 20%

commit v1 on v0

--- a/solution.py
+++ b/solution.py
@@ -355,7 +355,7 @@
     asked = lax.all_to_all(req.reshape(groups, 1, LANES), "corpus", split_axis=0, concat_axis=0, tiled=True)
     asked = asked.reshape(groups, LANES)
     slots = groups * capacity
-    parts = 4
+    parts = 2
     wanted = pl.pallas_call(
         functools.partial(fetch_kernel, capacity),
         grid=(parts,),
@@ -434,7 +434,7 @@
     own_hot = location[mine] - corpus_idx * per_owner
     tail = jnp.full((LANES - 3 * hot_each,), -1, jnp.int32)
     hot_loc = jnp.concatenate([own_hot, own_hot, own_hot, tail])[None, :]
-    step = 16
+    step = 32
     quarter = (per_owner // reps, feat)
     quarters = pl.pallas_call(
         functools.partial(slab_kernel, scale, capacity, hot_each),
@@ -467,7 +467,8 @@
         cost_estimate=pl.CostEstimate(flops=3_000_000_000, bytes_accessed=13_000_000, transcendentals=0),
         name="hot_sum",
     )(got, gathered)
-    hots = [hot_sum] + [turn(hot_sum, d) for d in range(1, reps)]
+    after, before = turn(hot_sum, 1), turn(hot_sum, reps - 1)
+    hots = [hot_sum, after, before, turn(before, reps - 1)]
     slab_grad = pl.pallas_call(
         functools.partial(finish_kernel, reps),
         out_shape=jax.ShapeDtypeStruct(quarter, F32),

time: 230 us -> 228 us (level)
  transfers between devices with their start and end apart: 9 -> 9, of which waited for: 5 -> 4; matrix products, arithmetic and copies ran while one was open for 8% -> 8% of each run, Pallas kernels for 20% -> 20%
where the time goes in v1:
time: 228 us; the launch traced here: 227 us
  waiting for transfers between devices  84.2 us (37%)
  Pallas kernels  62.6 us (27%)
  starting transfers between devices  24.8 us (11%)
  blocking collectives  19.7 us (9%)
  local copies, waits for them, and re-layouts  19 us (8%)
  between operations  14.2 us (6%)
    all_to_all x1, waiting for transfers between devices, shards(): lax.all_to_all(wanted.reshape(groups, capacity, feat), 'corpus', split_ax...  52.2 us
    all_to_all x1, blocking collectives, shards(): lax.all_to_all(req.reshape(groups, 1, LANES), 'corpus', split_axis=0, con...  19.7 us
    pallas_call x1, Pallas kernels, shards(): pl.pallas_call(count_kernel, out_shape=(jax.ShapeDtypeStruct((hot_total,...  18.5 us
    all_gather x1, waiting for transfers between devices, shards(): gathered = lax.all_gather(sent_rows, 'corpus', axis=0, tiled=False)  17.8 us
    gather x1, local copies, waits for them, and re-layouts, shards(): gathered.reshape(-1, feat)  14.2 us
    ppermute x6, waiting for transfers between devices, turn(): lax.ppermute(array, 'rep', [(r, (r + d) % reps) for r in range(reps)])  11.5 us
    ppermute x6, starting transfers between devices, turn(): lax.ppermute(array, 'rep', [(r, (r + d) % reps) for r in range(reps)])  10.1 us
    all_to_all x1, starting transfers between devices, shards(): got = lax.all_to_all(pay, 'corpus', split_axis=0, concat_axis=0, tiled=True)  8.07 us
  transfers between devices with their start and end apart: 9, of which 4 were waited for; matrix products, arithmetic and copies ran while one was open for 8% of the time, Pallas kernels for 20%

profile of v1, /device:TPU:6, one launch (start us, length us, event | category | flops | bytes accessed | tf_op | source)
XLA Modules:
  0.0 226.7 jit_solution(9673130632463484480)
XLA Ops:
  7.9 3.2 %prep.1 = bf16[160,768]{1,0:T(8,128)(2,1)} custom-call(s32[2]{0:T(128)} %pad_add_fusion.spot_ref, bf16[128,768]{1,0:T(8,128)(2,1)} %q_ref.5, s32[16,128]{1,0:T(8,128)} %bitcast.27, s32[512,128]{1,0:T(8,128)} %bitcast.23, bf16[1024,768]{1,0:T(8,128)(2,1)} %slab_ref.3), custom_call_target="tpu_custom_call" | custom-call | tf_op jit(solution)/shard_map/prep/pallas_call | solution.py:333
  11.1 6.2 %request.1 = (s32[64,128]{1,0:T(8,128)}, s32[16,128]{1,0:T(8,128)}, s32[64,128]{1,0:T(8,128)}) custom-call(s32[64,128]{1,0:T(8,128)} %bitcast.30, s32[1,2048]{1,0:T(1,128)} %bitcast.28, s32[512,128]{1,0:T(8,128)} %bitcast.24), custom_call_target="tpu_custom_call" | custom-call | tf_op jit(solution)/shard_map/request/pallas_call | solution.py:343
  17.3 19.7 %all_to_all.15 = s32[64,1,128]{2,1,0:T(1,128)} all-to-all(s32[64,1,128]{2,1,0:T(1,128)} %bitcast.32), channel_id=1, replica_groups=mesh['corpus'=64,'rep'=4] {'corpus'}, dimensions={0} | all-to-all | bytes 65536 | tf_op jit(solution)/shard_map/all_to_all | solution.py:355
  37.0 5.5 %fetch.1 = bf16[1536,768]{1,0:T(8,128)(2,1)} custom-call(s32[64,128]{1,0:T(8,128)} %bitcast.25, bf16[1024,768]{1,0:T(8,128)(2,1)} %slab_ref.3), custom_call_target="tpu_custom_call" | custom-call | tf_op jit(solution)/shard_map/fetch/pallas_call | solution.py:359
  42.5 6.6 %all-to-all-start.1 = ((bf16[64,24,768]{2,1,0:T(8,128)(2,1)}), bf16[64,24,768]{2,1,0:T(8,128)(2,1)S(1)}, u32[]{:S(2)}, u32[]{:S(2)}) async-start(bf16[64,24,768]{2,1,0:T(8,128)(2,1)} %bitcast.22), calls=%async_computation.1 | async-start | bytes 4718592 | tf_op jit(solution)/shard_map/all_to_all | solution.py:367
  49.1 18.5 %count.1 = (f32[2048,128]{1,0:T(8,128)}, f32[2048,128]{1,0:T(8,128)}, f32[16,128]{1,0:T(8,128)}) custom-call(s32[64,128]{1,0:T(8,128)} %bitcast.31, f32[64,128]{1,0:T(8,128)} %bitcast.33, s32[16,128]{1,0:T(8,128)} %bitcast.29, s32[64,128]{1,0:T(8,128)} %get-tuple-element.22.sel_ref), custom_call_target="tpu_custom_call" | custom-call | flops 80000000 | bytes 3000000 | tf_op jit(solution)/shard_map/count/pallas_call | solution.py:369
  67.6 52.2 %all-to-all-done.1 = bf16[64,24,768]{2,1,0:T(8,128)(2,1)S(1)} async-done(((bf16[64,24,768]{2,1,0:T(8,128)(2,1)}), bf16[64,24,768]{2,1,0:T(8,128)(2,1)S(1)}, u32[]{:S(2)}, u32[]{:S(2)}) %all-to-all-start.1) | async-done | bytes 2359328 | tf_op jit(solution)/shard_map/all_to_all | solution.py:367
  119.9 1.4 copy-done
  121.3 3.4 %cold.1.cold_ref = f32[8,128]{1,0:T(8,128)} custom-call(bf16[128,768]{1,0:T(8,128)(2,1)} %q_ref.5, bf16[1536,768]{1,0:T(8,128)(2,1)} %bitcast.20, s32[16,128]{1,0:T(8,128)} %get-tuple-element.21.place_ref), custom_call_target="tpu_custom_call" | custom-call | tf_op jit(solution)/shard_map/cold/pallas_call | solution.py:388
  124.7 17.8 %all-gather.3.cloned.1.call-done = bf16[10240,768]{1,0:T(8,128)(2,1)} async-done(((bf16[160,768]{1,0:T(8,128)(2,1)}), bf16[10240,768]{1,0:T(8,128)(2,1)}) %all-gather.3.cloned.1.call-update) | async-done | bytes 15728656 | tf_op jit(solution)/shard_map/all_gather | solution.py:342
  142.5 5.5 %score.1 = (f32[1,128]{1,0:T(1,128)}, bf16[64,40,128]{2,1,0:T(8,128)(2,1)}, f32[8,128]{1,0:T(8,128)}) custom-call(bf16[128,768]{1,0:T(8,128)(2,1)} %q_ref.5, bf16[64,160,768]{2,1,0:T(8,128)(2,1)} %bitcast.17, f32[8,128]{1,0:T(8,128)} %cold.1.cold_ref, f32[2048,128]{1,0:T(8,128)} %get-tuple-element.23.count_ref, f32[2048,128]{1,0:T(8,128)} %get-tuple-element.24.target_ref, ...), custom_call_target="tpu_custom_call" | custom-call | tf_op jit(solution)/shard_map/score/pallas_call | solution.py:395
  148.0 8.1 %all-to-all-start.2 = ((bf16[64,40,128]{2,1,0:T(8,128)(2,1)}), bf16[64,40,128]{2,1,0:T(8,128)(2,1)S(1)}, u32[]{:S(2)}, u32[]{:S(2)}) async-start(bf16[64,40,128]{2,1,0:T(8,128)(2,1)} %get-tuple-element.27.pay_ref), calls=%async_computation.2 | async-start | bytes 1310720 | tf_op jit(solution)/shard_map/all_to_all | solution.py:419
  158.5 14.2 %gather_fusion.1 = bf16[1536,768]{1,0:T(8,128)(2,1)} fusion(bf16[10240,768]{1,0:T(8,128)(2,1)} %all-gather.3.cloned.1.call-done, s32[2048]{0:T(1024)S(1)} %pad_clamp_fusion), kind=kCustom, calls=%fused_computation.1 | custom fusion | bytes 4724736 | tf_op jit(solution)/shard_map/gather | solution.py:431
  172.7 2.7 %all-to-all-done.2.pay_ref = bf16[64,40,128]{2,1,0:T(8,128)(2,1)S(1)} async-done(((bf16[64,40,128]{2,1,0:T(8,128)(2,1)}), bf16[64,40,128]{2,1,0:T(8,128)(2,1)S(1)}, u32[]{:S(2)}, u32[]{:S(2)}) %all-to-all-start.2) | async-done | bytes 655392 | tf_op jit(solution)/shard_map/all_to_all | solution.py:419
  175.4 0.8 copy-done.1
  176.2 6.6 %hot_sum.1.refs_0_ = f32[32,768]{1,0:T(8,128)} custom-call(bf16[64,40,128]{2,1,0:T(8,128)(2,1)} %copy-done.1, bf16[64,160,768]{2,1,0:T(8,128)(2,1)} %bitcast.18), custom_call_target="tpu_custom_call" | custom-call | flops 3000000000 | bytes 13000000 | tf_op jit(solution)/shard_map/hot_sum/pallas_call | solution.py:458
  182.9 3.1 %collective-permute-start.1 = (f32[32,768]{1,0:T(8,128)}, f32[32,768]{1,0:T(8,128)S(1)}, u32[]{:S(2)}, u32[]{:S(2)}) collective-permute-start(f32[32,768]{1,0:T(8,128)} %hot_sum.1.refs_0_), channel_id=1, source_target_pairs={{0,3},{1,0},{2,1},{3,2},{4,7},{5,4},{6,5},{7,6},{8,11},{9,8},{10,9... | collective-permute-start | bytes 294920 | tf_op jit(solution)/shard_map/ppermute | solution.py:455
  186.0 6.1 %slab_grad.1 = (f32[256,768]{1,0:T(8,128)}, bf16[256,768]{1,0:T(8,128)(2,1)}, bf16[256,768]{1,0:T(8,128)(2,1)}, bf16[256,768]{1,0:T(8,128)(2,1)}) custom-call(s32[2]{0:T(128)} %pad_add_fusion.spot_ref, bf16[64,40,128]{2,1,0:T(8,128)(2,1)} %copy-done.1, bf16[1536,768]{1,0:T(8,128)(2,1)} %gather_fusion.1, s32[1,1536]{1,0:T(1,128)} %reshape.82.loc_ref), custom_call_target="tpu_custom_call" | custom-call | tf_op jit(solution)/shard_map/slab_grad/pallas_call | solution.py:439
  192.7 1.1 collective-permute-start.4
  193.8 2.2 collective-permute-start.5
  196.0 3.2 %collective-permute-start.2 = (f32[32,768]{1,0:T(8,128)S(1)}, f32[32,768]{1,0:T(8,128)S(1)}, u32[]{:S(2)}, u32[]{:S(2)}) collective-permute-start(f32[32,768]{1,0:T(8,128)S(1)} %collective-permute-done.1.refs_2_), channel_id=1, source_target_pairs={{0,3},{1,0},{2,1},{3,2},{4,7},{5,4},{6,5},{7,6},{8,11},{9,8},{10,9... | collective-permute-start | bytes 294920 | tf_op jit(solution)/shard_map/ppermute | solution.py:455
  199.8 4.6 %query_grad.1 = f32[128,768]{1,0:T(8,128)} custom-call(bf16[64,160,768]{2,1,0:T(8,128)(2,1)} %bitcast.19, bf16[64,40,128]{2,1,0:T(8,128)(2,1)} %get-tuple-element.27.pay_ref, bf16[1536,768]{1,0:T(8,128)(2,1)} %bitcast.21, f32[8,128]{1,0:T(8,128)} %get-tuple-element.28.weight_ref, s32[16,128]{1,0:T(8,128)} %get-tuple-element.21.place_ref), custom_call_target="tpu_custom_call" | custom-call | flops 700000000 | bytes 7000000 | tf_op jit(solution)/shard_map/query_grad/pallas_call | solution.py:420
  204.4 11.5 %collective-permute-done.refs_1_ = f32[32,768]{1,0:T(8,128)S(1)} collective-permute-done((f32[32,768]{1,0:T(8,128)S(1)}, f32[32,768]{1,0:T(8,128)S(1)}, u32[]{:S(2)}, u32[]{:S(2)}) %collective-permute-start) | collective-permute-done | bytes 98336 | tf_op jit(solution)/shard_map/ppermute | solution.py:455
  217.0 2.8 %finish.1 = f32[256,768]{1,0:T(8,128)} custom-call(s32[2]{0:T(128)} %pad_add_fusion.spot_ref, s32[1,128]{1,0:T(1,128)} %add_bitcast_fusion.hot_loc_ref, f32[32,768]{1,0:T(8,128)} %hot_sum.1.refs_0_, f32[32,768]{1,0:T(8,128)} %copy-done.9, f32[32,768]{1,0:T(8,128)} %copy-done.8, f32[32,768]{1,0:T(8,128)} %copy-done.10, f32[256,768]{1,0:T(8,128)} %get-tuple-element.29.refs_4_, ...), custom_call_target="tpu_custom_call" | custom-call | tf_op jit(solution)/shard_map/finish/pallas_call | solution.py:472
  (42 shorter events, 5.4 us)
Async XLA Ops:
  7.2 135.4 %all-gather.3.cloned.1.call-start = ((), (), s32[]{:S(2)}) async-start(), calls=%async_computation.3 | async-start | bytes 15974400 | tf_op jit(solution)/shard_map/all_gather | solution.py:342
  42.5 77.4 %all-to-all-start.1 = ((bf16[64,24,768]{2,1,0:T(8,128)(2,1)}), bf16[64,24,768]{2,1,0:T(8,128)(2,1)S(1)}, u32[]{:S(2)}, u32[]{:S(2)}) async-start(bf16[64,24,768]{2,1,0:T(8,128)(2,1)} %bitcast.22), calls=%async_computation.1 | async-start | bytes 4718592 | tf_op jit(solution)/shard_map/all_to_all | solution.py:367
  119.9 1.4 copy-start
  142.5 14.4 %copy-start.2 = (s32[65536]{0:T(1024)S(1)}, s32[65536]{0:T(1024)}, u32[]{:S(2)}) copy-start(s32[65536]{0:T(1024)} %param.11) | copy-start | bytes 786436
  142.5 15.1 %copy-start.7 = (s32[64,1,128]{2,1,0:T(1,128)S(1)}, s32[64,1,128]{2,1,0:T(1,128)}, u32[]{:S(2)}) copy-start(s32[64,1,128]{2,1,0:T(1,128)} %all_to_all.15) | copy-start | bytes 98308
  148.0 27.4 %all-to-all-start.2 = ((bf16[64,40,128]{2,1,0:T(8,128)(2,1)}), bf16[64,40,128]{2,1,0:T(8,128)(2,1)S(1)}, u32[]{:S(2)}, u32[]{:S(2)}) async-start(bf16[64,40,128]{2,1,0:T(8,128)(2,1)} %get-tuple-element.27.pay_ref), calls=%async_computation.2 | async-start | bytes 1310720 | tf_op jit(solution)/shard_map/all_to_all | solution.py:419
  175.4 0.8 copy-start.1
  182.9 13.1 %copy-start.3 = (f32[32,768]{1,0:T(8,128)S(1)}, f32[32,768]{1,0:T(8,128)}, u32[]{:S(2)}) copy-start(f32[32,768]{1,0:T(8,128)} %hot_sum.1.refs_0_) | copy-start | bytes 294916
  182.9 13.1 %collective-permute-start.1 = (f32[32,768]{1,0:T(8,128)}, f32[32,768]{1,0:T(8,128)S(1)}, u32[]{:S(2)}, u32[]{:S(2)}) collective-permute-start(f32[32,768]{1,0:T(8,128)} %hot_sum.1.refs_0_), channel_id=1, source_target_pairs={{0,3},{1,0},{2,1},{3,2},{4,7},{5,4},{6,5},{7,6},{8,11},{9,8},{10,9... | collective-permute-start | bytes 294920 | tf_op jit(solution)/shard_map/ppermute | solution.py:455
  192.1 23.8 %collective-permute-start.3 = (bf16[256,768]{1,0:T(8,128)(2,1)}, bf16[256,768]{1,0:T(8,128)(2,1)S(1)}, u32[]{:S(2)}, u32[]{:S(2)}) collective-permute-start(bf16[256,768]{1,0:T(8,128)(2,1)} %get-tuple-element.30), channel_id=1, source_target_pairs={{0,2},{1,3},{2,0},{3,1},{4,6},{5,7},{6,4},{7,5},{8,10},{9,11},{10,... | collective-permute-start | bytes 1179656 | tf_op jit(solution)/shard_map/ppermute | solution.py:455
  192.7 23.2 %collective-permute-start.4 = (bf16[256,768]{1,0:T(8,128)(2,1)}, bf16[256,768]{1,0:T(8,128)(2,1)S(1)}, u32[]{:S(2)}, u32[]{:S(2)}) collective-permute-start(bf16[256,768]{1,0:T(8,128)(2,1)} %get-tuple-element.31), channel_id=1, source_target_pairs={{0,1},{1,2},{2,3},{3,0},{4,5},{5,6},{6,7},{7,4},{8,9},{9,10},{10,1... | collective-permute-start | bytes 1179656 | tf_op jit(solution)/shard_map/ppermute | solution.py:455
  193.8 22.2 %collective-permute-start.5 = (bf16[256,768]{1,0:T(8,128)(2,1)}, bf16[256,768]{1,0:T(8,128)(2,1)S(1)}, u32[]{:S(2)}, u32[]{:S(2)}) collective-permute-start(bf16[256,768]{1,0:T(8,128)(2,1)} %get-tuple-element.32), channel_id=1, source_target_pairs={{0,3},{1,0},{2,1},{3,2},{4,7},{5,4},{6,5},{7,6},{8,11},{9,8},{10,9... | collective-permute-start | bytes 1179656 | tf_op jit(solution)/shard_map/ppermute | solution.py:455
  195.9 19.9 %collective-permute-start = (f32[32,768]{1,0:T(8,128)S(1)}, f32[32,768]{1,0:T(8,128)S(1)}, u32[]{:S(2)}, u32[]{:S(2)}) collective-permute-start(f32[32,768]{1,0:T(8,128)S(1)} %copy-done.3), channel_id=1, source_target_pairs={{0,1},{1,2},{2,3},{3,0},{4,5},{5,6},{6,7},{7,4},{8,9},{9,10},{10,1... | collective-permute-start | bytes 294920 | tf_op jit(solution)/shard_map/ppermute | solution.py:455
  196.0 8.5 %copy-start.8 = (f32[32,768]{1,0:T(8,128)}, f32[32,768]{1,0:T(8,128)S(1)}, u32[]{:S(2)}) copy-start(f32[32,768]{1,0:T(8,128)S(1)} %collective-permute-done.1.refs_2_) | copy-start | bytes 294916
  196.0 19.9 %collective-permute-start.2 = (f32[32,768]{1,0:T(8,128)S(1)}, f32[32,768]{1,0:T(8,128)S(1)}, u32[]{:S(2)}, u32[]{:S(2)}) collective-permute-start(f32[32,768]{1,0:T(8,128)S(1)} %collective-permute-done.1.refs_2_), channel_id=1, source_target_pairs={{0,3},{1,0},{2,1},{3,2},{4,7},{5,4},{6,5},{7,6},{8,11},{9,8},{10,9... | collective-permute-start | bytes 294920 | tf_op jit(solution)/shard_map/ppermute | solution.py:455
  215.9 0.6 copy-start.9
  215.9 0.7 copy-start.10
  215.9 0.8 copy-start.4
  215.9 0.9 copy-start.5
  215.9 1.0 copy-start.6
Sparse Core Ops, SparseCore 0:
  11.3 131.1 all-gather.2
